TPU v7x, 256 devices: a whole 4x4x8 slice. The times are simulated.
256 devices in a mesh: rows: 16 (over z, core), cols: 16 (over y, x).
Axes of the slice: x: 4, y: 4, z: 8, core: 2. Of those that a mesh axis runs over, the one named last changes fastest.
Arguments:
- tensor: float32 [32, 2048, 2048], P(None, 'rows', 'cols'), may hold values from -819200 to 819200
- second_init: float32 [2048, 64], P('cols'), may hold values from -6 to 6
- third_init: float32 [32, 64], replicated, may hold values from -6 to 6
Outputs:
- first: float32 [2048, 64], P('rows')
- second: float32 [2048, 64], P('cols')
- third: float32 [32, 64], replicated
All inputs are finite; a program needn't handle non-finite values.
Results may differ from a plain program's by a relative error of at most 0.0003.
Values sent between devices are 32-bit elements; how exact they have to be, the bound alone decides.
No kernel may reach another device: no remote copies, remote signals or barrier semaphores. Data moves between devices by JAX's collectives and lax.ppermute only.
A program may use at most 64 MiB of HBM per device.

v0:
```python
import jax
import jax.numpy as jnp
from jax import lax
from jax.sharding import PartitionSpec as P

ITERS = 5
EPSILON = 1e-05
HIGHEST = lax.Precision.HIGHEST


def solve_right(rhs_rows, system):
    cholesky_low = jnp.linalg.cholesky(system)
    halfway = lax.linalg.triangular_solve(
        cholesky_low, rhs_rows, left_side=False, lower=True, transpose_a=True
    )
    return lax.linalg.triangular_solve(cholesky_low, halfway, left_side=False, lower=True)


def gram_local(factor):
    return jnp.dot(factor.T, factor, precision=HIGHEST, preferred_element_type=jnp.float32)


def settle(raw_share, total_rows):
    squares = lax.psum(jnp.sum(raw_share * raw_share, axis=0), ("rows", "cols"))
    col_scale = jnp.sqrt(squares / total_rows + EPSILON)
    normed = raw_share / col_scale
    gram_whole = lax.psum(gram_local(normed), ("rows", "cols"))
    return (col_scale, gram_whole)


def per_device(tensor, second_init, third_init):
    rows_here = tensor.shape[1]
    cols_here = tensor.shape[2]
    total_first = rows_here * lax.axis_size("rows")
    total_second = cols_here * lax.axis_size("cols")
    share_first = rows_here // lax.axis_size("cols")
    share_second = cols_here // lax.axis_size("rows")
    start_first = lax.axis_index("cols") * share_first
    start_second = lax.axis_index("rows") * share_second
    col_scale, gram_second = settle(
        lax.dynamic_slice_in_dim(second_init, start_second, share_second, 0), total_second
    )
    second = second_init / col_scale
    third = third_init
    gram_third = gram_local(third)
    first = None
    for sweep_index in range(ITERS):
        contract_first = lax.dot_general(
            second,
            tensor,
            (((0,), (2,)), ((), ())),
            precision=HIGHEST,
            preferred_element_type=jnp.float32,
        )
        system_first = gram_third * gram_second
        gram_first = None
        partial_first = jnp.einsum("rki,kr->ir", contract_first, third, precision=HIGHEST)
        mttkrp_first = lax.psum(partial_first, "cols")
        raw_block = solve_right(mttkrp_first, system_first)
        col_scale, gram_first = settle(
            lax.dynamic_slice_in_dim(raw_block, start_first, share_first, 0), total_first
        )
        carried_first = raw_block / col_scale
        contract_second = lax.dot_general(
            carried_first,
            tensor,
            (((0,), (1,)), ((), ())),
            precision=HIGHEST,
            preferred_element_type=jnp.float32,
        )
        partial_second = jnp.einsum("rkj,kr->jr", contract_second, third, precision=HIGHEST)
        outgoing = partial_second
        summed_second = lax.psum(outgoing, "rows")
        first = carried_first
        system_second = gram_third * gram_first
        raw_block = solve_right(summed_second, system_second)
        raw_part = lax.dynamic_slice_in_dim(raw_block, start_second, share_second, 0)
        col_scale, gram_second = settle(raw_part, total_second)
        carried_second = raw_block / col_scale
        partial_third = jnp.einsum("rkj,jr->kr", contract_second, carried_second, precision=HIGHEST)
        outgoing = partial_third
        summed_third = lax.psum(outgoing, ("rows", "cols"))
        second = carried_second
        third = solve_right(summed_third, gram_first * gram_second)
        gram_third = gram_local(third)
    return (first, second, third)


def solution(mesh):
    return jax.shard_map(
        per_device,
        mesh=mesh,
        in_specs=(P(None, "rows", "cols"), P("cols", None), P()),
        out_specs=(P("rows", None), P("cols", None), P()),
        check_vma=False,
    )
```

profile of v0, /device:TPU:1, one launch (start us, length us, event | category | flops | bytes accessed | tf_op | source)
XLA Modules:
  0.0 2455.2 jit_solution(10629154190226435686)
XLA Ops:
  1.7 81.4 %psum.259 = f32[64]{0:T(128)S(1)} all-reduce(f32[64]{0:T(128)S(1)} %multiply_reduce_fusion.10), channel_id=1, replica_groups=mesh['rows'=16,'cols'=16] {'rows','cols'}, use_global_device_ids=true, to_apply=%region_1.0 | all-reduce | flops 64 | bytes 512 | tf_op jit(solution)/shard_map/psum | solution.py:24
  85.1 72.8 %psum.260 = f32[64,64]{0,1:T(8,128)S(1)} all-reduce(f32[64,64]{0,1:T(8,128)S(1)} %fusion.163), channel_id=1, replica_groups=mesh['rows'=16,'cols'=16] {'rows','cols'}, use_global_device_ids=true, to_apply=%region_2.0 | all-reduce | flops 4096 | bytes 32768 | tf_op jit(solution)/shard_map/psum | solution.py:27
  233.2 86.1 %psum.262 = f32[64]{0:T(128)S(1)} all-reduce(f32[64]{0:T(128)S(1)} %multiply_reduce_fusion.9), channel_id=1, replica_groups=mesh['rows'=16,'cols'=16] {'rows','cols'}, use_global_device_ids=true, to_apply=%region_7.11 | all-reduce | flops 64 | bytes 512 | tf_op jit(solution)/shard_map/psum | solution.py:24
  319.6 73.9 %psum.263 = f32[64,64]{0,1:T(8,128)S(1)} all-reduce(f32[64,64]{0,1:T(8,128)S(1)} %fusion.160), channel_id=1, replica_groups=mesh['rows'=16,'cols'=16] {'rows','cols'}, use_global_device_ids=true, to_apply=%region_8.12 | all-reduce | flops 4096 | bytes 32768 | tf_op jit(solution)/shard_map/psum | solution.py:27
  453.3 76.4 %psum.265 = f32[64]{0:T(128)S(1)} all-reduce(f32[64]{0:T(128)S(1)} %multiply_reduce_fusion.8), channel_id=1, replica_groups=mesh['rows'=16,'cols'=16] {'rows','cols'}, use_global_device_ids=true, to_apply=%region_11.15 | all-reduce | flops 64 | bytes 512 | tf_op jit(solution)/shard_map/psum | solution.py:24
  532.2 74.2 %all-reduce.4 = (f32[32,64]{0,1:T(8,128)S(1)}, f32[64,64]{0,1:T(8,128)S(1)}) all-reduce(f32[32,64]{0,1:T(8,128)S(1)} %bitcast.444, f32[64,64]{0,1:T(8,128)S(1)} %fusion.157), channel_id=1, replica_groups=mesh['rows'=16,'cols'=16] {'rows','cols'}, use_global_device_ids=true, to_apply=%region_13.17 | all-reduce | flops 6144 | bytes 49152 | tf_op jit(solution)/shard_map/psum | solution.py:82
  635.5 56.8 %psum.268 = f32[128,64]{0,1:T(8,128)S(1)} all-reduce(f32[128,64]{0,1:T(8,128)S(1)} %bitcast.451), channel_id=1, replica_groups=mesh['rows'=16,'cols'=16] {'cols'}, use_global_device_ids=true, to_apply=%region_14.20 | all-reduce | flops 8192 | bytes 65536 | tf_op jit(solution)/shard_map/psum | solution.py:58
  692.9 85.3 %psum.269 = f32[64]{0:T(128)S(1)} all-reduce(f32[64]{0:T(128)S(1)} %multiply_reduce_fusion.7), channel_id=1, replica_groups=mesh['rows'=16,'cols'=16] {'rows','cols'}, use_global_device_ids=true, to_apply=%region_16.22 | all-reduce | flops 64 | bytes 512 | tf_op jit(solution)/shard_map/psum | solution.py:24
  778.5 74.9 %psum.270 = f32[64,64]{0,1:T(8,128)S(1)} all-reduce(f32[64,64]{0,1:T(8,128)S(1)} %fusion.155), channel_id=1, replica_groups=mesh['rows'=16,'cols'=16] {'rows','cols'}, use_global_device_ids=true, to_apply=%region_17.23 | all-reduce | flops 4096 | bytes 32768 | tf_op jit(solution)/shard_map/psum | solution.py:27
  912.2 76.4 %psum.272 = f32[64]{0:T(128)S(1)} all-reduce(f32[64]{0:T(128)S(1)} %multiply_reduce_fusion.6), channel_id=1, replica_groups=mesh['rows'=16,'cols'=16] {'rows','cols'}, use_global_device_ids=true, to_apply=%region_20.26 | all-reduce | flops 64 | bytes 512 | tf_op jit(solution)/shard_map/psum | solution.py:24
  991.2 74.1 %all-reduce.3 = (f32[32,64]{0,1:T(8,128)S(1)}, f32[64,64]{0,1:T(8,128)S(1)}) all-reduce(f32[32,64]{0,1:T(8,128)S(1)} %bitcast.445, f32[64,64]{0,1:T(8,128)S(1)} %fusion.152), channel_id=1, replica_groups=mesh['rows'=16,'cols'=16] {'rows','cols'}, use_global_device_ids=true, to_apply=%region_22.28 | all-reduce | flops 6144 | bytes 49152 | tf_op jit(solution)/shard_map/psum | solution.py:82
  1151.8 85.3 %psum.276 = f32[64]{0:T(128)S(1)} all-reduce(f32[64]{0:T(128)S(1)} %multiply_reduce_fusion.5), channel_id=1, replica_groups=mesh['rows'=16,'cols'=16] {'rows','cols'}, use_global_device_ids=true, to_apply=%region_25.31 | all-reduce | flops 64 | bytes 512 | tf_op jit(solution)/shard_map/psum | solution.py:24
  1237.3 74.7 %psum.277 = f32[64,64]{0,1:T(8,128)S(1)} all-reduce(f32[64,64]{0,1:T(8,128)S(1)} %fusion.150), channel_id=1, replica_groups=mesh['rows'=16,'cols'=16] {'rows','cols'}, use_global_device_ids=true, to_apply=%region_26.32 | all-reduce | flops 4096 | bytes 32768 | tf_op jit(solution)/shard_map/psum | solution.py:27
  1370.9 76.4 %psum.279 = f32[64]{0:T(128)S(1)} all-reduce(f32[64]{0:T(128)S(1)} %multiply_reduce_fusion.4), channel_id=1, replica_groups=mesh['rows'=16,'cols'=16] {'rows','cols'}, use_global_device_ids=true, to_apply=%region_29.35 | all-reduce | flops 64 | bytes 512 | tf_op jit(solution)/shard_map/psum | solution.py:24
  1449.8 74.3 %all-reduce.2 = (f32[32,64]{0,1:T(8,128)S(1)}, f32[64,64]{0,1:T(8,128)S(1)}) all-reduce(f32[32,64]{0,1:T(8,128)S(1)} %bitcast.446, f32[64,64]{0,1:T(8,128)S(1)} %fusion.147), channel_id=1, replica_groups=mesh['rows'=16,'cols'=16] {'rows','cols'}, use_global_device_ids=true, to_apply=%region_31.37 | all-reduce | flops 6144 | bytes 49152 | tf_op jit(solution)/shard_map/psum | solution.py:82
  1553.2 56.8 %psum.282 = f32[128,64]{0,1:T(8,128)S(1)} all-reduce(f32[128,64]{0,1:T(8,128)S(1)} %bitcast.455), channel_id=1, replica_groups=mesh['rows'=16,'cols'=16] {'cols'}, use_global_device_ids=true, to_apply=%region_32.38 | all-reduce | flops 8192 | bytes 65536 | tf_op jit(solution)/shard_map/psum | solution.py:58
  1610.6 85.3 %psum.283 = f32[64]{0:T(128)S(1)} all-reduce(f32[64]{0:T(128)S(1)} %multiply_reduce_fusion.3), channel_id=1, replica_groups=mesh['rows'=16,'cols'=16] {'rows','cols'}, use_global_device_ids=true, to_apply=%region_34.40 | all-reduce | flops 64 | bytes 512 | tf_op jit(solution)/shard_map/psum | solution.py:24
  1696.2 74.6 %psum.284 = f32[64,64]{0,1:T(8,128)S(1)} all-reduce(f32[64,64]{0,1:T(8,128)S(1)} %fusion.145), channel_id=1, replica_groups=mesh['rows'=16,'cols'=16] {'rows','cols'}, use_global_device_ids=true, to_apply=%region_35.41 | all-reduce | flops 4096 | bytes 32768 | tf_op jit(solution)/shard_map/psum | solution.py:27
  1829.7 76.4 %psum.286 = f32[64]{0:T(128)S(1)} all-reduce(f32[64]{0:T(128)S(1)} %multiply_reduce_fusion.2), channel_id=1, replica_groups=mesh['rows'=16,'cols'=16] {'rows','cols'}, use_global_device_ids=true, to_apply=%region_38.44 | all-reduce | flops 64 | bytes 512 | tf_op jit(solution)/shard_map/psum | solution.py:24
  1908.7 74.2 %all-reduce.1 = (f32[32,64]{0,1:T(8,128)S(1)}, f32[64,64]{0,1:T(8,128)S(1)}) all-reduce(f32[32,64]{0,1:T(8,128)S(1)} %bitcast.447, f32[64,64]{0,1:T(8,128)S(1)} %fusion.142), channel_id=1, replica_groups=mesh['rows'=16,'cols'=16] {'rows','cols'}, use_global_device_ids=true, to_apply=%region_40.46 | all-reduce | flops 6144 | bytes 49152 | tf_op jit(solution)/shard_map/psum | solution.py:82
  2069.3 85.3 %psum.290 = f32[64]{0:T(128)S(1)} all-reduce(f32[64]{0:T(128)S(1)} %multiply_reduce_fusion.1), channel_id=1, replica_groups=mesh['rows'=16,'cols'=16] {'rows','cols'}, use_global_device_ids=true, to_apply=%region_43.49 | all-reduce | flops 64 | bytes 512 | tf_op jit(solution)/shard_map/psum | solution.py:24
  2155.0 74.7 %psum.291 = f32[64,64]{0,1:T(8,128)S(1)} all-reduce(f32[64,64]{0,1:T(8,128)S(1)} %fusion.140), channel_id=1, replica_groups=mesh['rows'=16,'cols'=16] {'rows','cols'}, use_global_device_ids=true, to_apply=%region_44.50 | all-reduce | flops 4096 | bytes 32768 | tf_op jit(solution)/shard_map/psum | solution.py:27
  2288.5 76.4 %psum.293 = f32[64]{0:T(128)S(1)} all-reduce(f32[64]{0:T(128)S(1)} %multiply_reduce_fusion), channel_id=1, replica_groups=mesh['rows'=16,'cols'=16] {'rows','cols'}, use_global_device_ids=true, to_apply=%region_47.53 | all-reduce | flops 64 | bytes 512 | tf_op jit(solution)/shard_map/psum | solution.py:24
  2367.5 73.9 %all-reduce = (f32[32,64]{0,1:T(8,128)S(1)}, f32[64,64]{0,1:T(8,128)S(1)}) all-reduce(f32[32,64]{0,1:T(8,128)S(1)} %bitcast.448, f32[64,64]{0,1:T(8,128)S(1)} %fusion.138), channel_id=1, replica_groups=mesh['rows'=16,'cols'=16] {'rows','cols'}, use_global_device_ids=true, to_apply=%region_49.55 | all-reduce | flops 6144 | bytes 49152 | tf_op jit(solution)/shard_map/psum | solution.py:82
  (233 shorter events, 632.4 us)
Async XLA Ops:
  0.6 170.5 %copy-start = (f32[32,128,128]{2,1,0:T(8,128)S(1)}, f32[32,128,128]{2,1,0:T(8,128)}, u32[]{:S(2)}) copy-start(f32[32,128,128]{2,1,0:T(8,128)} %param.12) | copy-start | bytes 6291460
  2155.0 89.7 %copy-start.1 = (f32[128,64]{0,1:T(8,128)}, f32[128,64]{0,1:T(8,128)S(1)}, u32[]{:S(2)}) copy-start(f32[128,64]{0,1:T(8,128)S(1)} %broadcast_divide_fusion.1) | copy-start | bytes 98308
  2365.3 89.4 %copy-start.2 = (f32[128,64]{0,1:T(8,128)}, f32[128,64]{0,1:T(8,128)S(1)}, u32[]{:S(2)}) copy-start(f32[128,64]{0,1:T(8,128)S(1)} %broadcast_divide_fusion) | copy-start | bytes 98308
where the time goes:
time: 2470 us; the launch traced here: 2460 us
  blocking collectives  2210 us (89%)
  other arithmetic  185 us (7%)
  matrix products  57.5 us (2%)
    psum x11, blocking collectives, settle(): squares = lax.psum(jnp.sum(raw_share * raw_share, axis=0), ('rows', 'cols'))  891 us
    psum x6, blocking collectives, settle(): gram_whole = lax.psum(gram_local(normed), ('rows', 'cols'))  446 us
    psum x5, blocking collectives, per_device(): summed_third = lax.psum(outgoing, ('rows', 'cols'))  371 us
    psum x5, blocking collectives, per_device(): mttkrp_first = lax.psum(partial_first, 'cols')  284 us
    psum x5, blocking collectives, per_device(): summed_second = lax.psum(outgoing, 'rows')  218 us
    another operation x45, other arithmetic, solve_right(): cholesky_low = jnp.linalg.cholesky(system)  97.8 us
    another operation x30, other arithmetic, solve_right(): lax.linalg.triangular_solve(cholesky_low, halfway, left_side=False, lower...  83.2 us

commit v1 on v0

--- a/solution.py
+++ b/solution.py
@@ -6,6 +6,10 @@
 ITERS = 5
 EPSILON = 1e-05
 HIGHEST = lax.Precision.HIGHEST
+
+
+def reach_matrix(base_x, link_axis):
+    return lax.all_gather(base_x, link_axis).sum(axis=0)
 
 
 def solve_right(rhs_rows, system):
@@ -70,7 +74,7 @@
         )
         partial_second = jnp.einsum("rkj,kr->jr", contract_second, third, precision=HIGHEST)
         outgoing = partial_second
-        summed_second = lax.psum(outgoing, "rows")
+        summed_second = reach_matrix(outgoing, link_axis="rows")
         first = carried_first
         system_second = gram_third * gram_first
         raw_block = solve_right(summed_second, system_second)

time: 2470 us -> 2330 us (0.943)
  blocking collectives: 2210 us -> 2070 us
    psum x5 -> x0, blocking collectives: 218 us -> none  [per_device(): summed_second = lax.psum(outgoing, 'rows')]
    all_gather x0 -> x5, blocking collectives: none -> 87.2 us  [reach_matrix(): return lax.all_gather(base_x, link_axis).sum(axis=0)]
where the time goes in v1:
time: 2330 us; the launch traced here: 2310 us
  blocking collectives  2070 us (89%)
  other arithmetic  185 us (8%)
  matrix products  57.5 us (2%)
    psum x11, blocking collectives, settle(): squares = lax.psum(jnp.sum(raw_share * raw_share, axis=0), ('rows', 'cols'))  873 us
    psum x6, blocking collectives, settle(): gram_whole = lax.psum(gram_local(normed), ('rows', 'cols'))  446 us
    psum x5, blocking collectives, per_device(): summed_third = lax.psum(outgoing, ('rows', 'cols'))  374 us
    psum x5, blocking collectives, per_device(): mttkrp_first = lax.psum(partial_first, 'cols')  288 us
    another operation x45, other arithmetic, solve_right(): cholesky_low = jnp.linalg.cholesky(system)  97.8 us
    all_gather x5, blocking collectives, reach_matrix(): return lax.all_gather(base_x, link_axis).sum(axis=0)  87.2 us
    another operation x30, other arithmetic, solve_right(): lax.linalg.triangular_solve(cholesky_low, halfway, left_side=False, lower...  83.2 us

profile of v1, /device:TPU:1, one launch (start us, length us, event | category | flops | bytes accessed | tf_op | source)
XLA Modules:
  0.0 2314.8 jit_solution(11819328879103933585)
XLA Ops:
  1.7 81.4 %psum.224 = f32[64]{0:T(128)S(1)} all-reduce(f32[64]{0:T(128)S(1)} %multiply_reduce_fusion.10), channel_id=1, replica_groups=mesh['rows'=16,'cols'=16] {'rows','cols'}, use_global_device_ids=true, to_apply=%region_1.0 | all-reduce | flops 64 | bytes 512 | tf_op jit(solution)/shard_map/psum | solution.py:28
  85.1 72.8 %psum.225 = f32[64,64]{0,1:T(8,128)S(1)} all-reduce(f32[64,64]{0,1:T(8,128)S(1)} %fusion.163), channel_id=1, replica_groups=mesh['rows'=16,'cols'=16] {'rows','cols'}, use_global_device_ids=true, to_apply=%region_2.0 | all-reduce | flops 4096 | bytes 32768 | tf_op jit(solution)/shard_map/psum | solution.py:31
  233.2 86.1 %psum.227 = f32[64]{0:T(128)S(1)} all-reduce(f32[64]{0:T(128)S(1)} %multiply_reduce_fusion.9), channel_id=1, replica_groups=mesh['rows'=16,'cols'=16] {'rows','cols'}, use_global_device_ids=true, to_apply=%region_7.11 | all-reduce | flops 64 | bytes 512 | tf_op jit(solution)/shard_map/psum | solution.py:28
  319.6 73.9 %psum.228 = f32[64,64]{0,1:T(8,128)S(1)} all-reduce(f32[64,64]{0,1:T(8,128)S(1)} %fusion.160), channel_id=1, replica_groups=mesh['rows'=16,'cols'=16] {'rows','cols'}, use_global_device_ids=true, to_apply=%region_8.12 | all-reduce | flops 4096 | bytes 32768 | tf_op jit(solution)/shard_map/psum | solution.py:31
  427.4 73.4 %psum.229 = f32[64]{0:T(128)S(1)} all-reduce(f32[64]{0:T(128)S(1)} %multiply_reduce_fusion.8), channel_id=1, replica_groups=mesh['rows'=16,'cols'=16] {'rows','cols'}, use_global_device_ids=true, to_apply=%region_11.15 | all-reduce | flops 64 | bytes 512 | tf_op jit(solution)/shard_map/psum | solution.py:28
  503.4 74.8 %all-reduce.4 = (f32[32,64]{0,1:T(8,128)S(1)}, f32[64,64]{0,1:T(8,128)S(1)}) all-reduce(f32[32,64]{0,1:T(8,128)S(1)} %bitcast.479, f32[64,64]{0,1:T(8,128)S(1)} %fusion.157), channel_id=1, replica_groups=mesh['rows'=16,'cols'=16] {'rows','cols'}, use_global_device_ids=true, to_apply=%region_13.17 | all-reduce | flops 6144 | bytes 49152 | tf_op jit(solution)/shard_map/psum | solution.py:86
  665.5 84.6 %psum.233 = f32[64]{0:T(128)S(1)} all-reduce(f32[64]{0:T(128)S(1)} %multiply_reduce_fusion.7), channel_id=1, replica_groups=mesh['rows'=16,'cols'=16] {'rows','cols'}, use_global_device_ids=true, to_apply=%region_16.22 | all-reduce | flops 64 | bytes 512 | tf_op jit(solution)/shard_map/psum | solution.py:28
  750.4 74.9 %psum.234 = f32[64,64]{0,1:T(8,128)S(1)} all-reduce(f32[64,64]{0,1:T(8,128)S(1)} %fusion.155), channel_id=1, replica_groups=mesh['rows'=16,'cols'=16] {'rows','cols'}, use_global_device_ids=true, to_apply=%region_17.23 | all-reduce | flops 4096 | bytes 32768 | tf_op jit(solution)/shard_map/psum | solution.py:31
  858.3 73.4 %psum.235 = f32[64]{0:T(128)S(1)} all-reduce(f32[64]{0:T(128)S(1)} %multiply_reduce_fusion.6), channel_id=1, replica_groups=mesh['rows'=16,'cols'=16] {'rows','cols'}, use_global_device_ids=true, to_apply=%region_20.26 | all-reduce | flops 64 | bytes 512 | tf_op jit(solution)/shard_map/psum | solution.py:28
  934.3 74.7 %all-reduce.3 = (f32[32,64]{0,1:T(8,128)S(1)}, f32[64,64]{0,1:T(8,128)S(1)}) all-reduce(f32[32,64]{0,1:T(8,128)S(1)} %bitcast.480, f32[64,64]{0,1:T(8,128)S(1)} %fusion.152), channel_id=1, replica_groups=mesh['rows'=16,'cols'=16] {'rows','cols'}, use_global_device_ids=true, to_apply=%region_22.28 | all-reduce | flops 6144 | bytes 49152 | tf_op jit(solution)/shard_map/psum | solution.py:86
  1038.1 57.7 %psum.238 = f32[128,64]{0,1:T(8,128)S(1)} all-reduce(f32[128,64]{0,1:T(8,128)S(1)} %bitcast.486), channel_id=1, replica_groups=mesh['rows'=16,'cols'=16] {'cols'}, use_global_device_ids=true, to_apply=%region_23.29 | all-reduce | flops 8192 | bytes 65536 | tf_op jit(solution)/shard_map/psum | solution.py:62
  1096.4 84.6 %psum.239 = f32[64]{0:T(128)S(1)} all-reduce(f32[64]{0:T(128)S(1)} %multiply_reduce_fusion.5), channel_id=1, replica_groups=mesh['rows'=16,'cols'=16] {'rows','cols'}, use_global_device_ids=true, to_apply=%region_25.31 | all-reduce | flops 64 | bytes 512 | tf_op jit(solution)/shard_map/psum | solution.py:28
  1181.3 74.7 %psum.240 = f32[64,64]{0,1:T(8,128)S(1)} all-reduce(f32[64,64]{0,1:T(8,128)S(1)} %fusion.150), channel_id=1, replica_groups=mesh['rows'=16,'cols'=16] {'rows','cols'}, use_global_device_ids=true, to_apply=%region_26.32 | all-reduce | flops 4096 | bytes 32768 | tf_op jit(solution)/shard_map/psum | solution.py:31
  1288.9 73.5 %psum.241 = f32[64]{0:T(128)S(1)} all-reduce(f32[64]{0:T(128)S(1)} %multiply_reduce_fusion.4), channel_id=1, replica_groups=mesh['rows'=16,'cols'=16] {'rows','cols'}, use_global_device_ids=true, to_apply=%region_29.35 | all-reduce | flops 64 | bytes 512 | tf_op jit(solution)/shard_map/psum | solution.py:28
  1364.9 75.0 %all-reduce.2 = (f32[32,64]{0,1:T(8,128)S(1)}, f32[64,64]{0,1:T(8,128)S(1)}) all-reduce(f32[32,64]{0,1:T(8,128)S(1)} %bitcast.481, f32[64,64]{0,1:T(8,128)S(1)} %fusion.147), channel_id=1, replica_groups=mesh['rows'=16,'cols'=16] {'rows','cols'}, use_global_device_ids=true, to_apply=%region_31.37 | all-reduce | flops 6144 | bytes 49152 | tf_op jit(solution)/shard_map/psum | solution.py:86
  1468.9 57.7 %psum.244 = f32[128,64]{0,1:T(8,128)S(1)} all-reduce(f32[128,64]{0,1:T(8,128)S(1)} %bitcast.487), channel_id=1, replica_groups=mesh['rows'=16,'cols'=16] {'cols'}, use_global_device_ids=true, to_apply=%region_32.38 | all-reduce | flops 8192 | bytes 65536 | tf_op jit(solution)/shard_map/psum | solution.py:62
  1527.2 84.6 %psum.245 = f32[64]{0:T(128)S(1)} all-reduce(f32[64]{0:T(128)S(1)} %multiply_reduce_fusion.3), channel_id=1, replica_groups=mesh['rows'=16,'cols'=16] {'rows','cols'}, use_global_device_ids=true, to_apply=%region_34.40 | all-reduce | flops 64 | bytes 512 | tf_op jit(solution)/shard_map/psum | solution.py:28
  1612.1 74.6 %psum.246 = f32[64,64]{0,1:T(8,128)S(1)} all-reduce(f32[64,64]{0,1:T(8,128)S(1)} %fusion.145), channel_id=1, replica_groups=mesh['rows'=16,'cols'=16] {'rows','cols'}, use_global_device_ids=true, to_apply=%region_35.41 | all-reduce | flops 4096 | bytes 32768 | tf_op jit(solution)/shard_map/psum | solution.py:31
  1719.7 73.5 %psum.247 = f32[64]{0:T(128)S(1)} all-reduce(f32[64]{0:T(128)S(1)} %multiply_reduce_fusion.2), channel_id=1, replica_groups=mesh['rows'=16,'cols'=16] {'rows','cols'}, use_global_device_ids=true, to_apply=%region_38.44 | all-reduce | flops 64 | bytes 512 | tf_op jit(solution)/shard_map/psum | solution.py:28
  1795.7 74.8 %all-reduce.1 = (f32[32,64]{0,1:T(8,128)S(1)}, f32[64,64]{0,1:T(8,128)S(1)}) all-reduce(f32[32,64]{0,1:T(8,128)S(1)} %bitcast.482, f32[64,64]{0,1:T(8,128)S(1)} %fusion.142), channel_id=1, replica_groups=mesh['rows'=16,'cols'=16] {'rows','cols'}, use_global_device_ids=true, to_apply=%region_40.46 | all-reduce | flops 6144 | bytes 49152 | tf_op jit(solution)/shard_map/psum | solution.py:86
  1957.8 84.6 %psum.251 = f32[64]{0:T(128)S(1)} all-reduce(f32[64]{0:T(128)S(1)} %multiply_reduce_fusion.1), channel_id=1, replica_groups=mesh['rows'=16,'cols'=16] {'rows','cols'}, use_global_device_ids=true, to_apply=%region_43.49 | all-reduce | flops 64 | bytes 512 | tf_op jit(solution)/shard_map/psum | solution.py:28
  2042.8 74.7 %psum.252 = f32[64,64]{0,1:T(8,128)S(1)} all-reduce(f32[64,64]{0,1:T(8,128)S(1)} %fusion.140), channel_id=1, replica_groups=mesh['rows'=16,'cols'=16] {'rows','cols'}, use_global_device_ids=true, to_apply=%region_44.50 | all-reduce | flops 4096 | bytes 32768 | tf_op jit(solution)/shard_map/psum | solution.py:31
  2150.5 73.5 %psum.253 = f32[64]{0:T(128)S(1)} all-reduce(f32[64]{0:T(128)S(1)} %multiply_reduce_fusion), channel_id=1, replica_groups=mesh['rows'=16,'cols'=16] {'rows','cols'}, use_global_device_ids=true, to_apply=%region_47.53 | all-reduce | flops 64 | bytes 512 | tf_op jit(solution)/shard_map/psum | solution.py:28
  2226.5 74.5 %all-reduce = (f32[32,64]{0,1:T(8,128)S(1)}, f32[64,64]{0,1:T(8,128)S(1)}) all-reduce(f32[32,64]{0,1:T(8,128)S(1)} %bitcast.483, f32[64,64]{0,1:T(8,128)S(1)} %fusion.138), channel_id=1, replica_groups=mesh['rows'=16,'cols'=16] {'rows','cols'}, use_global_device_ids=true, to_apply=%region_49.55 | all-reduce | flops 6144 | bytes 49152 | tf_op jit(solution)/shard_map/psum | solution.py:86
  (243 shorter events, 504.8 us)
Async XLA Ops:
  0.6 170.5 %copy-start = (f32[32,128,128]{2,1,0:T(8,128)S(1)}, f32[32,128,128]{2,1,0:T(8,128)}, u32[]{:S(2)}) copy-start(f32[32,128,128]{2,1,0:T(8,128)} %param.12) | copy-start | bytes 6291460
  2042.8 89.6 %copy-start.1 = (f32[128,64]{0,1:T(8,128)}, f32[128,64]{0,1:T(8,128)S(1)}, u32[]{:S(2)}) copy-start(f32[128,64]{0,1:T(8,128)S(1)} %broadcast_divide_fusion.1) | copy-start | bytes 98308
  2224.3 90.0 %copy-start.2 = (f32[128,64]{0,1:T(8,128)}, f32[128,64]{0,1:T(8,128)S(1)}, u32[]{:S(2)}) copy-start(f32[128,64]{0,1:T(8,128)S(1)} %broadcast_divide_fusion) | copy-start | bytes 98308
